TPU v7x, 32 devices: a whole 2x2x4 slice. The times are simulated.
32 devices in a mesh: site: 8 (over y, x, core), scen: 4 (over z).
Axes of the slice: x: 2, y: 2, z: 4, core: 2. Of those that a mesh axis runs over, the one named last changes fastest.
Arguments:
- normals: bfloat16 [20480, 1344], P('site', 'scen'), may hold values from -6 to 6
- pattern: int32 [32, 40], replicated, may hold values from 0 to 79, as said below
- factor: bfloat16 [32, 40, 256, 256], P('site', None, 'scen'), may hold values from -0.0625 to 0.0625
- temporal: bfloat16 [168, 168], replicated, may hold values from -0.5 to 0.5
- capacity: float32 [8192], P('site'), may hold values from 0.05 to 0.4
- spread: float32 [8192], P('site'), may hold values from 0.2 to 0.8
- bus_map: int32 [8192], replicated, may hold values from 0 to 511
Outputs:
- bus_power: float32 [512, 1344], P('site', 'scen')
Inputs may be any that keep to these rules, and one draw needn't show every extreme that they name: `pattern`: each block row names 40 different column blocks. The 4 block rows of one index of site (rows k * 4 to (k + 1) * 4 - 1) name at most 5 different column blocks among those held by any one index of site (blocks j * 10 to (j + 1) * 10 - 1), and exactly 5 among those held by index k itself.
All inputs are finite; a program needn't handle non-finite values.
Results may differ from a plain program's by a relative error of at most 0.0013.
Values may be sent and summed in bfloat16 or wider, within the bound.
A program may use at most 192 MiB of HBM per device.

v0:
```python
import functools

import jax
import jax.numpy as jnp
from jax import lax
from jax.experimental import pallas as pl
from jax.experimental.pallas import tpu as pltpu
from jax.sharding import PartitionSpec as P

MAX_COLUMN_BLOCKS = 5
PAIR = 2
CHUNKS = 3
LANES = 128
VMEM_LIMIT = 67043328
MESH = pl.DeviceIdType.MESH


def kernel(
    chips,
    groups,
    slots,
    hours,
    pattern_ref,
    z_ref,
    f_ref,
    temporal_ref,
    capacity_ref,
    spreads_ref,
    buses_ref,
    out_ref,
    z_all,
    z_work,
    f_raw,
    f_sorted,
    f_all,
    s_send,
    s_own,
    s_all,
    s_sum,
    b_send,
    b_all,
    x_send,
    x_all,
    c_send,
    c_all,
    onehot,
    scale_ref,
    spread_ref,
    pos,
    need,
    ranks,
    gathered,
    tables,
    scalars,
    local_sem,
    zsend,
    zrecv,
    psend,
    precv,
    fsend,
    frecv,
    ssend,
    srecv,
    bsend,
    brecv,
    csend,
    crecv,
    xsend,
    xrecv,
):
    k = lax.axis_index("site")
    z = lax.axis_index("scen")
    q = k // PAIR
    c = k % PAIR
    other = q * PAIR + (PAIR - 1 - c)
    rows_here, nz, height, blk = f_ref.shape
    width, depth = z_ref.shape
    bounds = bounds_of(width)
    each = slots // chips
    scens = width // hours
    shared = b_send.shape[3]
    sites = chips * PAIR
    held = depth // blk
    lanes = pos.shape[1]
    rows = rows_here * height
    last = groups - 1

    z_load = pltpu.make_async_copy(z_ref, z_all.at[z, c], local_sem.at[0])
    z_load.start()
    f_load = pltpu.make_async_copy(f_ref, f_raw, local_sem.at[1])
    f_load.start()

    barrier = pltpu.get_barrier_semaphore()

    def peer(e):
        return (q + e) % chips

    for d in range(1, groups):
        pl.semaphore_signal(barrier, inc=1, device_id=(k, (z + d) % groups), device_id_type=MESH)
    for e in range(1, chips):
        pl.semaphore_signal(barrier, inc=1, device_id=(peer(e) * PAIR + c, z), device_id_type=MESH)
    pl.semaphore_signal(barrier, inc=1, device_id=(other, z), device_id_type=MESH)

    lane = lax.broadcasted_iota(jnp.int32, (1, lanes), 1)
    owner = jnp.zeros_like(lane)
    for j in range(1, sites):
        owner = owner + jnp.where(lane >= j * held, 1, 0)
    local = lane - owner * held
    found = jnp.zeros(pos.shape, jnp.int32)
    for t in range(nz):
        found = jnp.where(pattern_ref[:, t : t + 1] == lane, t + 1, found)
    pos[...] = found
    for i in range(sites):
        line = pos[i * rows_here : i * rows_here + 1, :]
        for r in range(1, rows_here):
            at = i * rows_here + r
            line = jnp.maximum(line, pos[at : at + 1, :])
        need[i : i + 1, :] = jnp.where(line > 0, 1, 0)
    wanted = need[...]
    before = jnp.zeros_like(wanted)
    for d in range(1, held):
        before = before + jnp.where(local >= d, pltpu.roll(wanted, d, 1), 0)
    ranks[...] = before

    half_rows = tables.shape[0] // 2
    column = lax.broadcasted_iota(jnp.int32, (half_rows, tables.shape[1]), 1)
    gathered[...] = jnp.zeros_like(gathered)
    for r in range(rows_here):
        gathered[0, r : r + 1, :] = pos[pl.ds(k * rows_here + r, 1), :]
    for i in range(chips):
        gathered[1, i : i + 1, :] = need[pl.ds(i * PAIR + c, 1), :]
        gathered[2, i : i + 1, :] = ranks[pl.ds(i * PAIR + c, 1), :]
    own_slot = owner * MAX_COLUMN_BLOCKS + ranks[pl.ds(k, 1), :]
    own_slot = jnp.where(need[pl.ds(k, 1), :] > 0, own_slot, -1)
    places = jnp.zeros(column.shape, jnp.int32)
    positions = gathered[0]
    for t in range(slots):
        at = jnp.sum(jnp.where(own_slot == t, positions, 0), axis=1, keepdims=True)
        places = jnp.where(column == t, at, places)
    tables[0:half_rows, :] = places - 1
    blocks = jnp.zeros(column.shape, jnp.int32)
    needs, orders = gathered[1], gathered[2]
    first = q * PAIR * held
    for half in range(PAIR):
        mine = jnp.where(owner == q * PAIR + half, needs, 0)
        for j in range(MAX_COLUMN_BLOCKS):
            hit = jnp.where(orders == j, mine, 0)
            at = jnp.sum(hit * (lane - first), axis=1, keepdims=True)
            blocks = jnp.where(column == half * MAX_COLUMN_BLOCKS + j, at, blocks)
    tables[half_rows:, :] = blocks
    t_load = pltpu.make_async_copy(tables, scalars, local_sem.at[2])
    t_load.start()

    narrow = capacity_ref.shape[1]
    narrow_lane = lax.broadcasted_iota(jnp.int32, (8, narrow), 1)
    offset = z * height

    def rows_of(ref, base):
        parts = []
        for start in range(0, rows, narrow):
            part = None
            for r in range(start // height, min((start + narrow) // height, rows_here)):
                line = ref[pl.ds(base + r * blk // narrow + offset // narrow, 1), :]
                line = jnp.broadcast_to(line, narrow_lane.shape)
                shift = (r * height - start + narrow - offset % narrow) % narrow
                line = pltpu.roll(line, shift, 1)
                if part is None:
                    part = line
                else:
                    part = jnp.where(narrow_lane >= r * height - start, line, part)
            parts.append(part[0:1])
        return jnp.concatenate(parts, axis=1) if len(parts) > 1 else parts[0]

    scale_ref[...] = rows_of(capacity_ref, 0)
    spread_ref[...] = rows_of(spreads_ref, 0)
    maps = rows_of(buses_ref, k * (rows_here * blk // narrow))
    bus_ids = lax.broadcasted_iota(jnp.int32, onehot.shape, 0)
    onehot[...] = jnp.where(bus_ids == maps, 1.0, 0.0).astype(onehot.dtype)
    t_load.wait()
    pl.semaphore_wait(barrier, groups - 1 + chips - 1 + 1)

    def piece(ch):
        return pl.ds(bounds[ch], bounds[ch + 1] - bounds[ch])

    def hop(g, ch, up, source=None):
        part = z_all.at[g, c, piece(ch)]
        return pltpu.make_async_remote_copy(
            src_ref=part if source is None else source,
            dst_ref=part,
            send_sem=zsend.at[up, g, ch],
            recv_sem=zrecv.at[g, ch],
            device_id=(k, z + 1 if up else z - 1),
            device_id_type=MESH,
        )

    def share(g, ch, source=None):
        part = z_all.at[g, c, piece(ch)]
        return pltpu.make_async_remote_copy(
            src_ref=part if source is None else source,
            dst_ref=part,
            send_sem=psend.at[g, ch],
            recv_sem=precv.at[g, ch],
            device_id=(other, z),
            device_id_type=MESH,
        )

    def came_in(g, ch):
        part = z_all.at[g, c, piece(ch)]
        return pltpu.make_async_remote_copy(
            src_ref=part,
            dst_ref=part,
            send_sem=psend.at[g, ch],
            recv_sem=zrecv.at[g, ch],
            device_id=(other, z),
            device_id_type=MESH,
        )

    def shared_in(g, ch):
        part = z_all.at[g, 1 - c, piece(ch)]
        return pltpu.make_async_remote_copy(
            src_ref=part,
            dst_ref=part,
            send_sem=psend.at[g, ch],
            recv_sem=precv.at[g, ch],
            device_id=(other, z),
            device_id_type=MESH,
        )

    for ch in range(CHUNKS):
        own = z_ref.at[piece(ch)]

        @pl.when(z < last)
        def _():
            hop(z, ch, 1, own).start()

        @pl.when(z > 0)
        def _():
            hop(z, ch, 0, own).start()

    for ch in range(CHUNKS):
        share(z, ch, z_ref.at[piece(ch)]).start()

    def relay(g, ch):
        came_in(g, ch).wait_recv()

        @pl.when(jnp.logical_and(g < z, z < last))
        def _():
            hop(g, ch, 1).start()

        @pl.when(jnp.logical_and(g > z, z > 0))
        def _():
            hop(g, ch, 0).start()

        share(g, ch).start()

    def arrivals(d, ch):
        @pl.when(z - d >= 0)
        def _():
            relay(z - d, ch)

        @pl.when(z + d <= last)
        def _():
            relay(z + d, ch)

    def f_copy(target, source):
        return pltpu.make_async_remote_copy(
            src_ref=f_sorted.at[target],
            dst_ref=f_all.at[source],
            send_sem=fsend.at[target],
            recv_sem=frecv.at[source],
            device_id=(target * PAIR + c, z),
            device_id_type=MESH,
        )

    f_load.wait()

    def sort_for(target, store):
        def one(s, carry):
            for r in range(rows_here):
                t = scalars[r, target * each + s]
                block = f_raw[r, jnp.maximum(t, 0)]
                if slots > nz:
                    block = jnp.where(t >= 0, block, jnp.zeros_like(block))
                store(s, r, block)
            return carry

        lax.fori_loop(0, each, one, 0)

    for e in range(1, chips):
        target = peer(e)

        def to_send(s, r, block):
            f_sorted[target, s, pl.ds(r * height, height), :] = block

        sort_for(target, to_send)
        f_copy(target, q).start()

    def to_own(s, r, block):
        f_all[q, s, pl.ds(r * height, height), :] = block

    sort_for(q, to_own)

    z_load.wait()

    for ch in range(CHUNKS):
        arrivals(1, ch)
    if groups > 2:
        arrivals(2, 0)
    for e in range(1, chips):
        f_copy(q, peer(e)).wait_recv()

    fewer = jnp.minimum(z, last - z)
    more = jnp.where(z < last - z, 1, -1)

    def group_at(p):
        near = jnp.where(p % 2 == 1, -((p + 1) // 2), (p + 1) // 2)
        far = more * (p - fewer)
        return z + jnp.where(p <= 2 * fewer, near, far)

    def s_copy(g, ch, slot, target, source):
        size = bounds[ch + 1] - bounds[ch]
        return pltpu.make_async_remote_copy(
            src_ref=s_send.at[slot, target, pl.ds(0, size)],
            dst_ref=s_all.at[g, ch, source, pl.ds(0, size)],
            send_sem=ssend.at[slot, target],
            recv_sem=srecv.at[g, ch, source],
            device_id=(target * PAIR + c, z),
            device_id_type=MESH,
        )

    def b_copy(g, s, target, source):
        return pltpu.make_async_remote_copy(
            src_ref=b_send.at[s, target],
            dst_ref=b_all.at[g, s, source],
            send_sem=bsend.at[s, target],
            recv_sem=brecv.at[g, s, source],
            device_id=(target * PAIR + c, z),
            device_id_type=MESH,
        )

    def x_copy(g):
        return pltpu.make_async_remote_copy(
            src_ref=x_send.at[g],
            dst_ref=x_all.at[g],
            send_sem=xsend.at[g],
            recv_sem=xrecv.at[g],
            device_id=(other, z),
            device_id_type=MESH,
        )

    def c_copy(g, source):
        return pltpu.make_async_remote_copy(
            src_ref=c_send.at[g],
            dst_ref=c_all.at[source],
            send_sem=csend.at[g],
            recv_sem=crecv.at[source],
            device_id=(k, g),
            device_id_type=MESH,
        )

    def multiply(g, ch, slot):
        size = bounds[ch + 1] - bounds[ch]
        shared_in(g, ch).wait_recv()
        for half in range(PAIR):
            for b in range(held):
                z_work[half * held + b, 0:size, :] = z_all[
                    g, half, piece(ch), b * blk : (b + 1) * blk
                ]

        def product(i):
            total = None
            for s in range(each):
                term = lax.dot_general(
                    z_work[scalars[half_rows + i, s], 0:size, :],
                    f_all[i, s],
                    (((1,), (1,)), ((), ())),
                    preferred_element_type=jnp.float32,
                )
                total = term if total is None else total + term
            return total

        def one(e, carry):
            target = peer(e)
            s_send[slot, target, 0:size, :] = product(target).astype(s_send.dtype)
            s_copy(g, ch, slot, target, q).start()
            return carry

        lax.fori_loop(1, chips, one, 0)
        s_own[slot, 0:size, :] = product(q)

    def finish(p, ch):
        g = group_at(p)
        size = bounds[ch + 1] - bounds[ch]
        total = s_own[(p * CHUNKS + ch) % 2, 0:size, :]
        for e in range(1, chips):
            s_copy(g, ch, 0, q, peer(e)).wait_recv()
            total = total + s_all[g, ch, peer(e), 0:size, :].astype(jnp.float32)
        s_sum[bounds[ch] : bounds[ch + 1], :] = total
        for s in range(scens):
            if not bounds[ch] < (s + 1) * hours <= bounds[ch + 1]:
                continue
            spatial = s_sum[s * hours : (s + 1) * hours, :].astype(jnp.bfloat16)
            weather = jnp.dot(temporal_ref[...], spatial, preferred_element_type=jnp.float32)
            spread = spread_ref[...]
            values = scale_ref[...] * jnp.exp(spread * weather - 0.5 * spread * spread)
            sums = lax.dot_general(
                values.astype(jnp.bfloat16),
                onehot[...],
                (((1,), (1,)), ((), ())),
                preferred_element_type=jnp.float32,
            ).astype(b_send.dtype)

            @pl.when(p > 0)
            def _():
                for e in range(1, chips):
                    b_copy(g, s, peer(e), q).wait_send()

            for i in range(chips):
                b_send[s, i] = sums[:, i * shared : (i + 1) * shared]
            for e in range(1, chips):
                b_copy(g, s, peer(e), q).start()
            b_all[g, s, q] = b_send[s, q]

    def exchange(p):
        g = group_at(p)
        parts = []
        for s in range(scens):
            for e in range(1, chips):
                b_copy(g, s, q, peer(e)).wait_recv()
            total = b_all[g, s, 0].astype(jnp.float32)
            for i in range(1, chips):
                total = total + b_all[g, s, i].astype(jnp.float32)
            parts.append(total)
        side = lax.broadcasted_iota(jnp.int32, parts[0].shape, 1) // (shared // PAIR)
        packed = []
        for core in range(PAIR):
            total = None
            for s in range(scens):
                shift = ((s - core) * (shared // PAIR)) % shared
                part = pltpu.roll(parts[s], shift, 1) if shift else parts[s]
                total = part if total is None else jnp.where(side == s, part, total)
            packed.append(total)
        x_send[g] = jnp.where(c == 0, packed[1], packed[0])
        x_copy(g).start()
        c_send[g] = jnp.where(c == 0, packed[0], packed[1])

    def forward(p):
        g = group_at(p)
        x_copy(g).wait_recv()
        total = c_send[g] + x_all[g]

        @pl.when(p == 0)
        def _():
            c_all[z] = total

        @pl.when(p > 0)
        def _():
            c_send[g] = total
            c_copy(g, z).start()

    def free(g, ch, slot):
        for e in range(1, chips):
            s_copy(g, ch, slot, peer(e), q).wait_send()

    def position(p, carry):
        g = group_at(p)
        for ch in range(CHUNKS):
            slot = (p * CHUNKS + ch) % 2
            if ch >= 2:
                free(g, ch - 2, slot)
            else:

                @pl.when(p > 0)
                def _():
                    free(g, ch + CHUNKS - 2, slot)

            multiply(g, ch, slot)
            if ch > 0:
                finish(p, ch - 1)

                @pl.when(p > 0)
                def _():
                    exchange(p - 1) if ch == 1 else forward(p - 1)

            else:

                @pl.when(p > 0)
                def _():
                    finish(p - 1, CHUNKS - 1)

            if ch + 1 < CHUNKS:

                @pl.when(p >= 2)
                def _():
                    arrivals(p, ch + 1)
            else:

                @pl.when(jnp.logical_and(p >= 2, p < last))
                def _():
                    arrivals(p + 1, 0)

        return carry

    lax.fori_loop(0, groups, position, 0)
    finish(last, CHUNKS - 1)
    exchange(last)
    forward(last)

    free(z, CHUNKS - 2, (groups * CHUNKS - 2) % 2)
    free(z, CHUNKS - 1, (groups * CHUNKS - 1) % 2)
    for e in range(1, chips):
        f_copy(peer(e), q).wait_send()
        for s in range(scens):
            b_copy(z, s, peer(e), q).wait_send()
    for g in range(groups):
        x_copy(g).wait_send()
        for ch in range(CHUNKS):
            share(g, ch).wait_send()

            @pl.when(jnp.logical_and(g <= z, z < last))
            def _():
                hop(g, ch, 1).wait_send()

            @pl.when(jnp.logical_and(g >= z, z > 0))
            def _():
                hop(g, ch, 0).wait_send()

    total = c_all[z]
    for d in range(1, groups):
        source = (z + d) % groups
        c_copy(z, source).wait_recv()
        total = total + c_all[source]
    turned = total.T
    share_of = shared // PAIR
    for s in range(scens):
        out_ref[:, s * hours : (s + 1) * hours] = turned[s * share_of : (s + 1) * share_of]
    for d in range(1, groups):
        c_copy((z + d) % groups, z).wait_send()


def bounds_of(width):
    small = width // 7
    large = (width - small) // (CHUNKS - 1)
    return [large * i for i in range(CHUNKS)] + [width]


def shards(normals, pattern, factor, temporal, capacity, spread, bus_map, buses):
    sites = lax.axis_size("site")
    groups = lax.axis_size("scen")
    depth, width = normals.shape
    rows_here, nz, height, blk = factor.shape
    hours = temporal.shape[0]
    scens = width // hours
    chips = sites // PAIR
    bounds = bounds_of(width)
    step = max(b - a for a, b in zip(bounds, bounds[1:]))
    slots = sites * MAX_COLUMN_BLOCKS
    each = slots // chips
    rows = rows_here * height
    shared = buses // chips
    block_count = depth // blk
    lanes = -(-block_count * sites // LANES) * LANES
    half_rows = -(-max(chips, rows_here) // 8) * 8

    bf16, f32, i32 = jnp.bfloat16, jnp.float32, jnp.int32
    dma = pltpu.SemaphoreType.DMA
    whole = pl.BlockSpec(memory_space=pltpu.VMEM)
    anywhere = pl.BlockSpec(memory_space=pl.ANY)
    return pl.pallas_call(
        functools.partial(kernel, chips, groups, slots, hours),
        out_shape=jax.ShapeDtypeStruct((buses // sites, width), f32),
        in_specs=[whole, anywhere, anywhere, whole, whole, whole, whole],
        out_specs=whole,
        scratch_shapes=[
            pltpu.VMEM((groups, PAIR, width, depth), bf16),
            pltpu.VMEM((PAIR * block_count, step, blk), bf16),
            pltpu.VMEM((rows_here, nz, height, blk), bf16),
            pltpu.VMEM((chips, each, rows, blk), bf16),
            pltpu.VMEM((chips, each, rows, blk), bf16),
            pltpu.VMEM((2, chips, step, rows), bf16),
            pltpu.VMEM((2, step, rows), f32),
            pltpu.VMEM((groups, CHUNKS, chips, step, rows), bf16),
            pltpu.VMEM((width, rows), f32),
            pltpu.VMEM((scens, chips, hours, shared), bf16),
            pltpu.VMEM((groups, scens, chips, hours, shared), bf16),
            pltpu.VMEM((groups, hours, shared), f32),
            pltpu.VMEM((groups, hours, shared), f32),
            pltpu.VMEM((groups, hours, shared), f32),
            pltpu.VMEM((groups, hours, shared), f32),
            pltpu.VMEM((buses, rows), bf16),
            pltpu.VMEM((1, rows), f32),
            pltpu.VMEM((1, rows), f32),
            pltpu.VMEM((pattern.shape[0], lanes), i32),
            pltpu.VMEM((sites, lanes), i32),
            pltpu.VMEM((sites, lanes), i32),
            pltpu.VMEM((3, half_rows, lanes), i32),
            pltpu.VMEM((2 * half_rows, LANES), i32),
            pltpu.SMEM((2 * half_rows, LANES), i32),
            dma((3,)),
            dma((2, groups, CHUNKS)),
            dma((groups, CHUNKS)),
            dma((groups, CHUNKS)),
            dma((groups, CHUNKS)),
            dma((chips,)),
            dma((chips,)),
            dma((2, chips)),
            dma((groups, CHUNKS, chips)),
            dma((scens, chips)),
            dma((groups, scens, chips)),
            dma((groups,)),
            dma((groups,)),
            dma((groups,)),
            dma((groups,)),
        ],
        compiler_params=pltpu.CompilerParams(
            collective_id=0, has_side_effects=True, vmem_limit_bytes=VMEM_LIMIT
        ),
    )(
        pattern,
        normals.T,
        factor,
        temporal,
        capacity.reshape(-1, LANES),
        spread.reshape(-1, LANES),
        bus_map.reshape(-1, LANES),
    )


def solution(mesh):
    placed = (P("site", "scen"), P(), P("site", None, "scen", None), P(), P("site"), P("site"), P())
    sites = mesh.shape["site"]

    def whole(normals, pattern, factor, temporal, capacity, spread, bus_map):
        buses = factor.shape[0] * factor.shape[3] // 16

        def body(*args):
            return shards(*args, buses)

        return jax.shard_map(
            body, mesh=mesh, in_specs=placed, out_specs=P("site", "scen"), check_vma=False
        )(normals, pattern, factor, temporal, capacity, spread, bus_map)

    return whole
```

profile of v0, /device:TPU:0, one launch (start us, length us, event | category | flops | bytes accessed | tf_op | source)
XLA Modules:
  0.0 137.9 jit_solution(16756364182679841977)
XLA Ops:
  0.0 136.4 %shard_map.73 = f32[64,336]{1,0:T(8,128)} custom-call(s32[32,40]{1,0:T(8,128)} %pattern_ref.1, bf16[336,2560]{1,0:T(8,128)(2,1)} %bitcast.4, bf16[4,40,64,256]{3,2,1,0:T(8,128)(2,1)} %f_ref.1, bf16[168,168]{1,0:T(8,128)(2,1)} %temporal_ref.1, f32[8,128]{1,0:T(8,128)} %bitcast.6, f32[8,128]{1,0:T(8,128)} %bitcast.7, s32[64,128]{1,0:T(8,128)} %bitcast.5), custom_call_target="tpu_custom_call" | custom-call | tf_op jit(solution)/shard_map/pallas_call | solution.py:569
  136.4 1.5 %copy.9 = f32[64,336]{1,0:T(8,128)} copy(f32[64,336]{1,0:T(8,128)} %shard_map.73) | data formatting | bytes 172032
where the time goes:
time: 138 us
  Pallas kernels  136 us (99%)
  local copies, waits for them, and re-layouts  1.54 us (1%)
    pallas_call x1, Pallas kernels, shards(): pl.pallas_call(functools.partial(kernel, chips, groups, slots, hours), ou...  136 us

commit v1 on v0

--- a/solution.py
+++ b/solution.py
@@ -20,14 +20,20 @@
     groups,
     slots,
     hours,
-    pattern_ref,
+    pattern_hbm,
     z_ref,
     f_ref,
+    temporal_hbm,
+    capacity_hbm,
+    spreads_hbm,
+    buses_hbm,
+    near_ref,
+    far_ref,
+    pattern_ref,
     temporal_ref,
     capacity_ref,
     spreads_ref,
     buses_ref,
-    out_ref,
     z_all,
     z_work,
     f_raw,
@@ -39,10 +45,10 @@
     s_sum,
     b_send,
     b_all,
-    x_send,
-    x_all,
     c_send,
     c_all,
+    c_mid,
+    c_sum,
     onehot,
     scale_ref,
     spread_ref,
@@ -65,8 +71,8 @@
     brecv,
     csend,
     crecv,
-    xsend,
-    xrecv,
+    mrecv,
+    meet,
 ):
     k = lax.axis_index("site")
     z = lax.axis_index("scen")
@@ -78,28 +84,129 @@
     bounds = bounds_of(width)
     each = slots // chips
     scens = width // hours
-    shared = b_send.shape[3]
+    share_of = near_ref.shape[0]
+    shared = share_of * PAIR
+    packed_rows = b_send.shape[2]
     sites = chips * PAIR
     held = depth // blk
     lanes = pos.shape[1]
     rows = rows_here * height
     last = groups - 1
 
+    bits = [1 << i for i in range(chips.bit_length() - 1)]
+
+    def across(bit):
+        return q + bit - 2 * bit * ((q // bit) % 2)
+
+    barrier = pltpu.get_barrier_semaphore()
+
+    def peer(e):
+        return (q + e) % chips
+
+    def greet(device):
+        pl.semaphore_signal(barrier, inc=1, device_id=device, device_id_type=MESH)
+
+    @pl.when(z < last)
+    def _():
+        greet((k, z + 1))
+
+    @pl.when(z > 0)
+    def _():
+        greet((k, z - 1))
+
+    greet((other, z))
+    for bit in bits:
+        greet((across(bit) * PAIR + c, z))
+
+    small = [
+        (pattern_hbm, pattern_ref),
+        (temporal_hbm, temporal_ref),
+        (capacity_hbm, capacity_ref),
+        (spreads_hbm, spreads_ref),
+        (buses_hbm, buses_ref),
+    ]
+    loads = [
+        pltpu.make_async_copy(source, target, local_sem.at[3 + i])
+        for i, (source, target) in enumerate(small)
+    ]
+    for load in loads:
+        load.start()
+    ends = jnp.where(z < last, 1, 0) + jnp.where(z > 0, 1, 0)
+    pl.semaphore_wait(barrier, 1 + len(bits) + ends)
+
+    def piece(ch):
+        return pl.ds(bounds[ch], bounds[ch + 1] - bounds[ch])
+
+    def hop(g, ch, up, source=None):
+        part = z_all.at[g, c, piece(ch)]
+        return pltpu.make_async_remote_copy(
+            src_ref=part if source is None else source,
+            dst_ref=part,
+            send_sem=zsend.at[up, g, ch],
+            recv_sem=zrecv.at[g, ch],
+            device_id=(k, z + 1 if up else z - 1),
+            device_id_type=MESH,
+        )
+
+    def share(g, ch, source=None):
+        part = z_all.at[g, c, piece(ch)]
+        return pltpu.make_async_remote_copy(
+            src_ref=part if source is None else source,
+            dst_ref=part,
+            send_sem=psend.at[g, ch],
+            recv_sem=precv.at[g, ch],
+            device_id=(other, z),
+            device_id_type=MESH,
+        )
+
+    def came_in(g, ch):
+        part = z_all.at[g, c, piece(ch)]
+        return pltpu.make_async_remote_copy(
+            src_ref=part,
+            dst_ref=part,
+            send_sem=psend.at[g, ch],
+            recv_sem=zrecv.at[g, ch],
+            device_id=(other, z),
+            device_id_type=MESH,
+        )
+
+    def shared_in(g, ch):
+        part = z_all.at[g, 1 - c, piece(ch)]
+        return pltpu.make_async_remote_copy(
+            src_ref=part,
+            dst_ref=part,
+            send_sem=psend.at[g, ch],
+            recv_sem=precv.at[g, ch],
+            device_id=(other, z),
+            device_id_type=MESH,
+        )
+
+    for ch in range(CHUNKS):
+        own = z_ref.at[piece(ch)]
+
+        @pl.when(z < last)
+        def _():
+            hop(z, ch, 1, own).start()
+
+        @pl.when(z > 0)
+        def _():
+            hop(z, ch, 0, own).start()
+
+    for ch in range(CHUNKS):
+        share(z, ch, z_ref.at[piece(ch)]).start()
+
+    for i, bit in enumerate(bits[:-1]):
+        pl.semaphore_signal(
+            meet.at[i], inc=1, device_id=(across(bit) * PAIR + c, z), device_id_type=MESH
+        )
+        pl.semaphore_wait(meet.at[i], 1)
+
     z_load = pltpu.make_async_copy(z_ref, z_all.at[z, c], local_sem.at[0])
     z_load.start()
     f_load = pltpu.make_async_copy(f_ref, f_raw, local_sem.at[1])
     f_load.start()
-
-    barrier = pltpu.get_barrier_semaphore()
-
-    def peer(e):
-        return (q + e) % chips
-
-    for d in range(1, groups):
-        pl.semaphore_signal(barrier, inc=1, device_id=(k, (z + d) % groups), device_id_type=MESH)
-    for e in range(1, chips):
-        pl.semaphore_signal(barrier, inc=1, device_id=(peer(e) * PAIR + c, z), device_id_type=MESH)
-    pl.semaphore_signal(barrier, inc=1, device_id=(other, z), device_id_type=MESH)
+    for load in loads:
+        load.wait()
 
     lane = lax.broadcasted_iota(jnp.int32, (1, lanes), 1)
     owner = jnp.zeros_like(lane)
@@ -177,68 +284,6 @@
     bus_ids = lax.broadcasted_iota(jnp.int32, onehot.shape, 0)
     onehot[...] = jnp.where(bus_ids == maps, 1.0, 0.0).astype(onehot.dtype)
     t_load.wait()
-    pl.semaphore_wait(barrier, groups - 1 + chips - 1 + 1)
-
-    def piece(ch):
-        return pl.ds(bounds[ch], bounds[ch + 1] - bounds[ch])
-
-    def hop(g, ch, up, source=None):
-        part = z_all.at[g, c, piece(ch)]
-        return pltpu.make_async_remote_copy(
-            src_ref=part if source is None else source,
-            dst_ref=part,
-            send_sem=zsend.at[up, g, ch],
-            recv_sem=zrecv.at[g, ch],
-            device_id=(k, z + 1 if up else z - 1),
-            device_id_type=MESH,
-        )
-
-    def share(g, ch, source=None):
-        part = z_all.at[g, c, piece(ch)]
-        return pltpu.make_async_remote_copy(
-            src_ref=part if source is None else source,
-            dst_ref=part,
-            send_sem=psend.at[g, ch],
-            recv_sem=precv.at[g, ch],
-            device_id=(other, z),
-            device_id_type=MESH,
-        )
-
-    def came_in(g, ch):
-        part = z_all.at[g, c, piece(ch)]
-        return pltpu.make_async_remote_copy(
-            src_ref=part,
-            dst_ref=part,
-            send_sem=psend.at[g, ch],
-            recv_sem=zrecv.at[g, ch],
-            device_id=(other, z),
-            device_id_type=MESH,
-        )
-
-    def shared_in(g, ch):
-        part = z_all.at[g, 1 - c, piece(ch)]
-        return pltpu.make_async_remote_copy(
-            src_ref=part,
-            dst_ref=part,
-            send_sem=psend.at[g, ch],
-            recv_sem=precv.at[g, ch],
-            device_id=(other, z),
-            device_id_type=MESH,
-        )
-
-    for ch in range(CHUNKS):
-        own = z_ref.at[piece(ch)]
-
-        @pl.when(z < last)
-        def _():
-            hop(z, ch, 1, own).start()
-
-        @pl.when(z > 0)
-        def _():
-            hop(z, ch, 0, own).start()
-
-    for ch in range(CHUNKS):
-        share(z, ch, z_ref.at[piece(ch)]).start()
 
     def relay(g, ch):
         came_in(g, ch).wait_recv()
@@ -276,12 +321,14 @@
 
     def sort_for(target, store):
         def one(s, carry):
+            blocks = []
             for r in range(rows_here):
                 t = scalars[r, target * each + s]
                 block = f_raw[r, jnp.maximum(t, 0)]
                 if slots > nz:
                     block = jnp.where(t >= 0, block, jnp.zeros_like(block))
-                store(s, r, block)
+                blocks.append(block)
+            store(s, jnp.concatenate(blocks, axis=0).T)
             return carry
 
         lax.fori_loop(0, each, one, 0)
@@ -289,14 +336,14 @@
     for e in range(1, chips):
         target = peer(e)
 
-        def to_send(s, r, block):
-            f_sorted[target, s, pl.ds(r * height, height), :] = block
+        def to_send(s, tile):
+            f_sorted[target, s] = tile
 
         sort_for(target, to_send)
         f_copy(target, q).start()
 
-    def to_own(s, r, block):
-        f_all[q, s, pl.ds(r * height, height), :] = block
+    def to_own(s, tile):
+        f_all[q, s] = tile
 
     sort_for(q, to_own)
 
@@ -334,29 +381,50 @@
             dst_ref=b_all.at[g, s, source],
             send_sem=bsend.at[s, target],
             recv_sem=brecv.at[g, s, source],
-            device_id=(target * PAIR + c, z),
-            device_id_type=MESH,
-        )
-
-    def x_copy(g):
-        return pltpu.make_async_remote_copy(
-            src_ref=x_send.at[g],
-            dst_ref=x_all.at[g],
-            send_sem=xsend.at[g],
-            recv_sem=xrecv.at[g],
-            device_id=(other, z),
-            device_id_type=MESH,
-        )
-
-    def c_copy(g, source):
-        return pltpu.make_async_remote_copy(
-            src_ref=c_send.at[g],
-            dst_ref=c_all.at[source],
-            send_sem=csend.at[g],
-            recv_sem=crecv.at[source],
+            device_id=(target, z),
+            device_id_type=MESH,
+        )
+
+    def seat(e):
+        return (k + e) % sites
+
+    def c_copy(g, s, source):
+        return pltpu.make_async_remote_copy(
+            src_ref=c_send.at[g, s],
+            dst_ref=c_all.at[s, source],
+            send_sem=csend.at[g, s],
+            recv_sem=crecv.at[s, source],
             device_id=(k, g),
             device_id_type=MESH,
         )
+
+    beside = (1, last - 1)
+
+    def is_end(plane):
+        return jnp.logical_or(plane == 0, plane == last)
+
+    def inner(plane):
+        return jnp.logical_and(plane > 0, plane < last)
+
+    def m_copy(end, s, source):
+        return pltpu.make_async_remote_copy(
+            src_ref=c_send.at[end * last, s],
+            dst_ref=c_mid.at[end, s, source],
+            send_sem=csend.at[end * last, s],
+            recv_sem=mrecv.at[end, s, source],
+            device_id=(k, beside[end]),
+            device_id_type=MESH,
+        )
+
+    side = lax.broadcasted_iota(jnp.int32, (packed_rows, shared), 1) // share_of
+
+    def pack(block, core):
+        top, bottom = block[:packed_rows], block[hours - packed_rows :]
+        if core:
+            top = pltpu.roll(top, share_of, 1)
+        else:
+            bottom = pltpu.roll(bottom, share_of, 1)
+        return jnp.where(side == 0, top, bottom)
 
     def multiply(g, ch, slot):
         size = bounds[ch + 1] - bounds[ch]
@@ -373,7 +441,7 @@
                 term = lax.dot_general(
                     z_work[scalars[half_rows + i, s], 0:size, :],
                     f_all[i, s],
-                    (((1,), (1,)), ((), ())),
+                    (((1,), (0,)), ((), ())),
                     preferred_element_type=jnp.float32,
                 )
                 total = term if total is None else total + term
@@ -408,59 +476,53 @@
                 onehot[...],
                 (((1,), (1,)), ((), ())),
                 preferred_element_type=jnp.float32,
-            ).astype(b_send.dtype)
+            )
 
             @pl.when(p > 0)
             def _():
-                for e in range(1, chips):
-                    b_copy(g, s, peer(e), q).wait_send()
+                for e in range(1, sites):
+                    b_copy(g, s, seat(e), k).wait_send()
 
             for i in range(chips):
-                b_send[s, i] = sums[:, i * shared : (i + 1) * shared]
-            for e in range(1, chips):
-                b_copy(g, s, peer(e), q).start()
-            b_all[g, s, q] = b_send[s, q]
-
-    def exchange(p):
+                block = sums[:, i * shared : (i + 1) * shared]
+                for core in range(PAIR):
+                    b_send[s, i * PAIR + core] = pack(block, core).astype(b_send.dtype)
+            for e in range(1, sites):
+                b_copy(g, s, seat(e), k).start()
+            b_all[g, s, k] = b_send[s, k]
+
+    def forward(p, s):
         g = group_at(p)
-        parts = []
-        for s in range(scens):
-            for e in range(1, chips):
-                b_copy(g, s, q, peer(e)).wait_recv()
-            total = b_all[g, s, 0].astype(jnp.float32)
-            for i in range(1, chips):
-                total = total + b_all[g, s, i].astype(jnp.float32)
-            parts.append(total)
-        side = lax.broadcasted_iota(jnp.int32, parts[0].shape, 1) // (shared // PAIR)
-        packed = []
-        for core in range(PAIR):
-            total = None
-            for s in range(scens):
-                shift = ((s - core) * (shared // PAIR)) % shared
-                part = pltpu.roll(parts[s], shift, 1) if shift else parts[s]
-                total = part if total is None else jnp.where(side == s, part, total)
-            packed.append(total)
-        x_send[g] = jnp.where(c == 0, packed[1], packed[0])
-        x_copy(g).start()
-        c_send[g] = jnp.where(c == 0, packed[0], packed[1])
-
-    def forward(p):
-        g = group_at(p)
-        x_copy(g).wait_recv()
-        total = c_send[g] + x_all[g]
+        for e in range(1, sites):
+            b_copy(g, s, k, seat(e)).wait_recv()
+        total = b_all[g, s, 0].astype(jnp.float32)
+        for i in range(1, sites):
+            total = total + b_all[g, s, i].astype(jnp.float32)
 
         @pl.when(p == 0)
         def _():
-            c_all[z] = total
+            c_all[s, z] = total
 
         @pl.when(p > 0)
         def _():
-            c_send[g] = total
-            c_copy(g, z).start()
+            c_send[g, s] = total
+
+            @pl.when(jnp.logical_or(is_end(z), inner(g)))
+            def _():
+                c_copy(g, s, z).start()
+
+            for end, near in enumerate(beside):
+
+                @pl.when(jnp.logical_and(inner(z), jnp.logical_and(g == end * last, z != near)))
+                def _():
+                    m_copy(end, s, z).start()
 
     def free(g, ch, slot):
         for e in range(1, chips):
             s_copy(g, ch, slot, peer(e), q).wait_send()
+
+    def done_in(s):
+        return next(ch for ch in range(CHUNKS) if (s + 1) * hours <= bounds[ch + 1])
 
     def position(p, carry):
         g = group_at(p)
@@ -475,67 +537,109 @@
                     free(g, ch + CHUNKS - 2, slot)
 
             multiply(g, ch, slot)
+            for s in range(scens):
+                at = done_in(s) + 3
+                if at % CHUNKS == ch:
+
+                    @pl.when(p >= at // CHUNKS)
+                    def _():
+                        forward(p - at // CHUNKS, s)
+
             if ch > 0:
                 finish(p, ch - 1)
-
-                @pl.when(p > 0)
-                def _():
-                    exchange(p - 1) if ch == 1 else forward(p - 1)
-
             else:
 
                 @pl.when(p > 0)
                 def _():
                     finish(p - 1, CHUNKS - 1)
 
-            if ch + 1 < CHUNKS:
-
-                @pl.when(p >= 2)
+            step = ch + 1
+            if step < CHUNKS:
+
+                @pl.when(p > 2)
                 def _():
-                    arrivals(p, ch + 1)
+                    arrivals(p, step)
             else:
 
                 @pl.when(jnp.logical_and(p >= 2, p < last))
                 def _():
                     arrivals(p + 1, 0)
 
+            if groups > 2 and ch in (CHUNKS - 2, CHUNKS - 1):
+                early, part = (0, CHUNKS - 2) if ch == CHUNKS - 1 else (1, CHUNKS - 1)
+
+                @pl.when(p == early)
+                def _():
+                    arrivals(2, part)
+
         return carry
 
     lax.fori_loop(0, groups, position, 0)
-    finish(last, CHUNKS - 1)
-    exchange(last)
-    forward(last)
+    for at in range(CHUNKS, CHUNKS + 3):
+        if at == CHUNKS:
+            finish(last, CHUNKS - 1)
+        for s in range(scens):
+            if done_in(s) + 3 == at:
+                forward(last, s)
+
+    for g in range(groups):
+        for ch in range(CHUNKS):
+            share(g, ch).wait_send()
+
+            @pl.when(jnp.logical_and(g <= z, z < last))
+            def _():
+                hop(g, ch, 1).wait_send()
+
+            @pl.when(jnp.logical_and(g >= z, z > 0))
+            def _():
+                hop(g, ch, 0).wait_send()
+
+    for end, near in enumerate(beside):
+
+        @pl.when(jnp.logical_and(inner(z), z == near))
+        def _():
+            for s in range(scens):
+                total = c_send[end * last, s]
+                for source in range(1, last):
+                    if source != near:
+                        m_copy(end, s, source).wait_recv()
+                        total = total + c_mid[end, s, source]
+                c_send[end * last, s] = total
+                c_copy(end * last, s, z).start()
+
+    def unpack(packed, s, ref):
+        rest = pltpu.roll(packed[2 * packed_rows - hours :], share_of, 1)
+        whole = jnp.concatenate([packed, rest], axis=0)
+        ref[:, s * hours : (s + 1) * hours] = whole.T[:share_of]
+
+    for s in range(scens):
+        unpack(c_all[s, z], s, near_ref)
+        c_sum[s] = jnp.zeros_like(c_sum[s])
+    for d in range(1, groups):
+        source = (z + d) % groups
+        direct = jnp.logical_or(inner(z), is_end(source))
+        for end, near in enumerate(beside):
+            direct = jnp.logical_or(direct, jnp.logical_and(z == end * last, source == near))
+
+        @pl.when(direct)
+        def _():
+            for s in range(scens):
+                c_copy(z, s, source).wait_recv()
+                c_sum[s] = c_sum[s] + c_all[s, source]
+
+    for s in range(scens):
+        unpack(c_sum[s], s, far_ref)
 
     free(z, CHUNKS - 2, (groups * CHUNKS - 2) % 2)
     free(z, CHUNKS - 1, (groups * CHUNKS - 1) % 2)
     for e in range(1, chips):
         f_copy(peer(e), q).wait_send()
-        for s in range(scens):
-            b_copy(z, s, peer(e), q).wait_send()
-    for g in range(groups):
-        x_copy(g).wait_send()
-        for ch in range(CHUNKS):
-            share(g, ch).wait_send()
-
-            @pl.when(jnp.logical_and(g <= z, z < last))
-            def _():
-                hop(g, ch, 1).wait_send()
-
-            @pl.when(jnp.logical_and(g >= z, z > 0))
-            def _():
-                hop(g, ch, 0).wait_send()
-
-    total = c_all[z]
-    for d in range(1, groups):
-        source = (z + d) % groups
-        c_copy(z, source).wait_recv()
-        total = total + c_all[source]
-    turned = total.T
-    share_of = shared // PAIR
     for s in range(scens):
-        out_ref[:, s * hours : (s + 1) * hours] = turned[s * share_of : (s + 1) * share_of]
-    for d in range(1, groups):
-        c_copy((z + d) % groups, z).wait_send()
+        for e in range(1, sites):
+            b_copy(z, s, seat(e), k).wait_send()
+    for s in range(scens):
+        for d in range(1, groups):
+            c_copy((z + d) % groups, s, z).wait_send()
 
 
 def bounds_of(width):
@@ -558,6 +662,7 @@
     each = slots // chips
     rows = rows_here * height
     shared = buses // chips
+    packed_rows = (hours // 2 + 7) // 8 * 8
     block_count = depth // blk
     lanes = -(-block_count * sites // LANES) * LANES
     half_rows = -(-max(chips, rows_here) // 8) * 8
@@ -566,27 +671,32 @@
     dma = pltpu.SemaphoreType.DMA
     whole = pl.BlockSpec(memory_space=pltpu.VMEM)
     anywhere = pl.BlockSpec(memory_space=pl.ANY)
-    return pl.pallas_call(
+    near, far = pl.pallas_call(
         functools.partial(kernel, chips, groups, slots, hours),
-        out_shape=jax.ShapeDtypeStruct((buses // sites, width), f32),
-        in_specs=[whole, anywhere, anywhere, whole, whole, whole, whole],
-        out_specs=whole,
+        out_shape=[jax.ShapeDtypeStruct((buses // sites, width), f32)] * 2,
+        in_specs=[anywhere] * 7,
+        out_specs=[whole] * 2,
         scratch_shapes=[
+            pltpu.VMEM(pattern.shape, i32),
+            pltpu.VMEM(temporal.shape, bf16),
+            pltpu.VMEM((capacity.size // LANES, LANES), f32),
+            pltpu.VMEM((spread.size // LANES, LANES), f32),
+            pltpu.VMEM((bus_map.size // LANES, LANES), i32),
             pltpu.VMEM((groups, PAIR, width, depth), bf16),
             pltpu.VMEM((PAIR * block_count, step, blk), bf16),
             pltpu.VMEM((rows_here, nz, height, blk), bf16),
-            pltpu.VMEM((chips, each, rows, blk), bf16),
-            pltpu.VMEM((chips, each, rows, blk), bf16),
+            pltpu.VMEM((chips, each, blk, rows), bf16),
+            pltpu.VMEM((chips, each, blk, rows), bf16),
             pltpu.VMEM((2, chips, step, rows), bf16),
             pltpu.VMEM((2, step, rows), f32),
             pltpu.VMEM((groups, CHUNKS, chips, step, rows), bf16),
             pltpu.VMEM((width, rows), f32),
-            pltpu.VMEM((scens, chips, hours, shared), bf16),
-            pltpu.VMEM((groups, scens, chips, hours, shared), bf16),
-            pltpu.VMEM((groups, hours, shared), f32),
-            pltpu.VMEM((groups, hours, shared), f32),
-            pltpu.VMEM((groups, hours, shared), f32),
-            pltpu.VMEM((groups, hours, shared), f32),
+            pltpu.VMEM((scens, sites, packed_rows, shared), bf16),
+            pltpu.VMEM((groups, scens, sites, packed_rows, shared), bf16),
+            pltpu.VMEM((groups, scens, packed_rows, shared), f32),
+            pltpu.VMEM((scens, groups, packed_rows, shared), f32),
+            pltpu.VMEM((2, scens, groups, packed_rows, shared), f32),
+            pltpu.VMEM((scens, packed_rows, shared), f32),
             pltpu.VMEM((buses, rows), bf16),
             pltpu.VMEM((1, rows), f32),
             pltpu.VMEM((1, rows), f32),
@@ -596,7 +706,7 @@
             pltpu.VMEM((3, half_rows, lanes), i32),
             pltpu.VMEM((2 * half_rows, LANES), i32),
             pltpu.SMEM((2 * half_rows, LANES), i32),
-            dma((3,)),
+            dma((8,)),
             dma((2, groups, CHUNKS)),
             dma((groups, CHUNKS)),
             dma((groups, CHUNKS)),
@@ -605,12 +715,12 @@
             dma((chips,)),
             dma((2, chips)),
             dma((groups, CHUNKS, chips)),
-            dma((scens, chips)),
-            dma((groups, scens, chips)),
-            dma((groups,)),
-            dma((groups,)),
-            dma((groups,)),
-            dma((groups,)),
+            dma((scens, sites)),
+            dma((groups, scens, sites)),
+            dma((groups, scens)),
+            dma((scens, groups)),
+            dma((2, scens, groups)),
+            pltpu.SemaphoreType.REGULAR((max(chips.bit_length() - 2, 1),)),
         ],
         compiler_params=pltpu.CompilerParams(
             collective_id=0, has_side_effects=True, vmem_limit_bytes=VMEM_LIMIT
@@ -624,6 +734,7 @@
         spread.reshape(-1, LANES),
         bus_map.reshape(-1, LANES),
     )
+    return near + far
 
 
 def solution(mesh):

time: 138 us -> 136 us (0.986)
  Pallas kernels: 136 us -> 134 us
  other arithmetic: 0 us -> 1.59 us
  local copies, waits for them, and re-layouts: 1.54 us -> 0 us
    pallas_call x1, Pallas kernels: 136 us -> 134 us  [shards(): pl.pallas_call(functools.partial(kernel, chips, groups, slots, hours), ou...]
    add x0 -> x1, other arithmetic: none -> 1.59 us  [shards(): return near + far]
    unnamed x1 -> x0, local copies, waits for them, and re-layouts: 1.54 us -> none
where the time goes in v1:
time: 136 us
  Pallas kernels  134 us (99%)
  other arithmetic  1.59 us (1%)
    pallas_call x1, Pallas kernels, shards(): pl.pallas_call(functools.partial(kernel, chips, groups, slots, hours), ou...  134 us

profile of v1, /device:TPU:0, one launch (start us, length us, event | category | flops | bytes accessed | tf_op | source)
XLA Modules:
  0.0 135.5 jit_solution(18056075430797520033)
XLA Ops:
  0.0 133.9 %shard_map.73 = (f32[64,336]{1,0:T(8,128)}, f32[64,336]{1,0:T(8,128)}) custom-call(s32[32,40]{1,0:T(8,128)} %pattern_hbm.1, bf16[336,2560]{1,0:T(8,128)(2,1)} %bitcast.4, bf16[4,40,64,256]{3,2,1,0:T(8,128)(2,1)} %f_ref.1, bf16[168,168]{1,0:T(8,128)(2,1)} %temporal_hbm.1, f32[8,128]{1,0:T(8,128)} %bitcast.6, f32[8,128]{1,0:T(8,128)} %bitcast.7, s32[64,128]{1,0:T(8,128)} %bitcast.5), custom_call_target="tpu_custom_call" | custom-call | tf_op jit(solution)/shard_map/pallas_call | solution.py:674
  133.9 1.6 %add.3 = f32[64,336]{1,0:T(8,128)} add(f32[64,336]{1,0:T(8,128)} %get-tuple-element.7, f32[64,336]{1,0:T(8,128)} %get-tuple-element.8) | non-fusion elementwise | flops 21504 | bytes 258048 | tf_op jit(solution)/shard_map/add | solution.py:737

commit v2 on v1

--- a/solution.py
+++ b/solution.py
@@ -1,4 +1,5 @@
 import functools
+import math
 
 import jax
 import jax.numpy as jnp
@@ -12,6 +13,7 @@
 CHUNKS = 3
 LANES = 128
 VMEM_LIMIT = 67043328
+VMEM_MARGIN = 3 * 1024 * 1024
 MESH = pl.DeviceIdType.MESH
 
 
@@ -183,12 +185,13 @@
 
     for ch in range(CHUNKS):
         own = z_ref.at[piece(ch)]
-
-        @pl.when(z < last)
+        late = ch == CHUNKS - 1
+
+        @pl.when(z < (last - 1 if late else last))
         def _():
             hop(z, ch, 1, own).start()
 
-        @pl.when(z > 0)
+        @pl.when(z > (1 if late else 0))
         def _():
             hop(z, ch, 0, own).start()
 
@@ -307,6 +310,17 @@
         def _():
             relay(z + d, ch)
 
+        if ch == CHUNKS - 1:
+            own = z_ref.at[piece(ch)]
+
+            @pl.when(jnp.logical_and(d == last - 1, z == 1))
+            def _():
+                hop(z, ch, 0, own).start()
+
+            @pl.when(jnp.logical_and(d == last - 1, z == last - 1))
+            def _():
+                hop(z, ch, 1, own).start()
+
     def f_copy(target, source):
         return pltpu.make_async_remote_copy(
             src_ref=f_sorted.at[target],
@@ -349,10 +363,14 @@
 
     z_load.wait()
 
-    for ch in range(CHUNKS):
+    for ch in range(CHUNKS - 1):
         arrivals(1, ch)
-    if groups > 2:
-        arrivals(2, 0)
+
+    @pl.when(jnp.logical_and(z > 0, z < last))
+    def _():
+        arrivals(1, CHUNKS - 1)
+
+    arrivals(2, 0)
     for e in range(1, chips):
         f_copy(q, peer(e)).wait_recv()
 
@@ -456,18 +474,21 @@
         lax.fori_loop(1, chips, one, 0)
         s_own[slot, 0:size, :] = product(q)
 
+    def lane_of(p):
+        return jnp.where(p == 1, 1, 0)
+
     def finish(p, ch):
         g = group_at(p)
         size = bounds[ch + 1] - bounds[ch]
-        total = s_own[(p * CHUNKS + ch) % 2, 0:size, :]
+        total = s_own[ch, 0:size, :]
         for e in range(1, chips):
             s_copy(g, ch, 0, q, peer(e)).wait_recv()
             total = total + s_all[g, ch, peer(e), 0:size, :].astype(jnp.float32)
-        s_sum[bounds[ch] : bounds[ch + 1], :] = total
+        s_sum[lane_of(p), bounds[ch] : bounds[ch + 1], :] = total
         for s in range(scens):
             if not bounds[ch] < (s + 1) * hours <= bounds[ch + 1]:
                 continue
-            spatial = s_sum[s * hours : (s + 1) * hours, :].astype(jnp.bfloat16)
+            spatial = s_sum[lane_of(p), s * hours : (s + 1) * hours, :].astype(jnp.bfloat16)
             weather = jnp.dot(temporal_ref[...], spatial, preferred_element_type=jnp.float32)
             spread = spread_ref[...]
             values = scale_ref[...] * jnp.exp(spread * weather - 0.5 * spread * spread)
@@ -524,34 +545,46 @@
     def done_in(s):
         return next(ch for ch in range(CHUNKS) if (s + 1) * hours <= bounds[ch + 1])
 
+    final = CHUNKS - 1
+
+    def stage(p, ch):
+        g = group_at(p)
+
+        @pl.when(p > 0)
+        def _():
+            free(g, ch, ch)
+
+        multiply(g, ch, ch)
+
     def position(p, carry):
-        g = group_at(p)
         for ch in range(CHUNKS):
-            slot = (p * CHUNKS + ch) % 2
-            if ch >= 2:
-                free(g, ch - 2, slot)
+            if ch == final:
+
+                @pl.when(p != 1)
+                def _():
+                    stage(p, ch)
+
             else:
-
-                @pl.when(p > 0)
-                def _():
-                    free(g, ch + CHUNKS - 2, slot)
-
-            multiply(g, ch, slot)
+                stage(p, ch)
             for s in range(scens):
                 at = done_in(s) + 3
                 if at % CHUNKS == ch:
-
-                    @pl.when(p >= at // CHUNKS)
+                    back = at // CHUNKS
+                    ready = p >= back
+                    if done_in(s) == final:
+                        ready = jnp.logical_and(ready, p != 1 + back)
+
+                    @pl.when(ready)
                     def _():
-                        forward(p - at // CHUNKS, s)
+                        forward(p - back, s)
 
             if ch > 0:
                 finish(p, ch - 1)
             else:
 
-                @pl.when(p > 0)
+                @pl.when(jnp.logical_and(p > 0, p != 2))
                 def _():
-                    finish(p - 1, CHUNKS - 1)
+                    finish(p - 1, final)
 
             step = ch + 1
             if step < CHUNKS:
@@ -565,22 +598,33 @@
                 def _():
                     arrivals(p + 1, 0)
 
-            if groups > 2 and ch in (CHUNKS - 2, CHUNKS - 1):
-                early, part = (0, CHUNKS - 2) if ch == CHUNKS - 1 else (1, CHUNKS - 1)
-
-                @pl.when(p == early)
-                def _():
-                    arrivals(2, part)
+            for part in range(1, CHUNKS):
+                if 2 * part % CHUNKS == ch:
+
+                    @pl.when(p == 2 * part // CHUNKS)
+                    def _():
+                        arrivals(2, part)
 
         return carry
 
     lax.fori_loop(0, groups, position, 0)
-    for at in range(CHUNKS, CHUNKS + 3):
-        if at == CHUNKS:
-            finish(last, CHUNKS - 1)
-        for s in range(scens):
-            if done_in(s) + 3 == at:
-                forward(last, s)
+    finish(last, final)
+
+    @pl.when(is_end(z))
+    def _():
+        arrivals(1, final)
+
+    for s in range(scens):
+        if done_in(s) < final and done_in(s) + 3 >= CHUNKS:
+            forward(last, s)
+    stage(1, final)
+    for s in range(scens):
+        if done_in(s) == final:
+            forward(last, s)
+    finish(1, final)
+    for s in range(scens):
+        if done_in(s) == final:
+            forward(1, s)
 
     for g in range(groups):
         for ch in range(CHUNKS):
@@ -615,23 +659,22 @@
     for s in range(scens):
         unpack(c_all[s, z], s, near_ref)
         c_sum[s] = jnp.zeros_like(c_sum[s])
-    for d in range(1, groups):
-        source = (z + d) % groups
-        direct = jnp.logical_or(inner(z), is_end(source))
-        for end, near in enumerate(beside):
-            direct = jnp.logical_or(direct, jnp.logical_and(z == end * last, source == near))
-
-        @pl.when(direct)
-        def _():
-            for s in range(scens):
+    for s in range(scens):
+        for d in range(1, groups):
+            source = (z + d) % groups
+            direct = jnp.logical_or(inner(z), is_end(source))
+            for end, near in enumerate(beside):
+                direct = jnp.logical_or(direct, jnp.logical_and(z == end * last, source == near))
+
+            @pl.when(direct)
+            def _():
                 c_copy(z, s, source).wait_recv()
                 c_sum[s] = c_sum[s] + c_all[s, source]
 
-    for s in range(scens):
         unpack(c_sum[s], s, far_ref)
 
-    free(z, CHUNKS - 2, (groups * CHUNKS - 2) % 2)
-    free(z, CHUNKS - 1, (groups * CHUNKS - 1) % 2)
+    for ch in range(CHUNKS):
+        free(z, ch, ch)
     for e in range(1, chips):
         f_copy(peer(e), q).wait_send()
     for s in range(scens):
@@ -643,9 +686,8 @@
 
 
 def bounds_of(width):
-    small = width // 7
-    large = (width - small) // (CHUNKS - 1)
-    return [large * i for i in range(CHUNKS)] + [width]
+    unit = width // 21
+    return [0, 8 * unit, 17 * unit, width]
 
 
 def shards(normals, pattern, factor, temporal, capacity, spread, bus_map, buses):
@@ -670,69 +712,81 @@
     bf16, f32, i32 = jnp.bfloat16, jnp.float32, jnp.int32
     dma = pltpu.SemaphoreType.DMA
     whole = pl.BlockSpec(memory_space=pltpu.VMEM)
-    anywhere = pl.BlockSpec(memory_space=pl.ANY)
+    anywhere = pl.BlockSpec(memory_space=pltpu.HBM)
+    scratch = [
+        pltpu.VMEM(pattern.shape, i32),
+        pltpu.VMEM(temporal.shape, bf16),
+        pltpu.VMEM((capacity.size // LANES, LANES), f32),
+        pltpu.VMEM((spread.size // LANES, LANES), f32),
+        pltpu.VMEM((bus_map.size // LANES, LANES), i32),
+        pltpu.VMEM((groups, PAIR, width, depth), bf16),
+        pltpu.VMEM((PAIR * block_count, step, blk), bf16),
+        pltpu.VMEM((rows_here, nz, height, blk), bf16),
+        pltpu.VMEM((chips, each, blk, rows), bf16),
+        pltpu.VMEM((chips, each, blk, rows), bf16),
+        pltpu.VMEM((CHUNKS, chips, step, rows), bf16),
+        pltpu.VMEM((CHUNKS, step, rows), f32),
+        pltpu.VMEM((groups, CHUNKS, chips, step, rows), bf16),
+        pltpu.VMEM((2, width, rows), f32),
+        pltpu.VMEM((scens, sites, packed_rows, shared), bf16),
+        pltpu.VMEM((groups, scens, sites, packed_rows, shared), bf16),
+        pltpu.VMEM((groups, scens, packed_rows, shared), f32),
+        pltpu.VMEM((scens, groups, packed_rows, shared), f32),
+        pltpu.VMEM((2, scens, groups, packed_rows, shared), f32),
+        pltpu.VMEM((scens, packed_rows, shared), f32),
+        pltpu.VMEM((buses, rows), bf16),
+        pltpu.VMEM((1, rows), f32),
+        pltpu.VMEM((1, rows), f32),
+        pltpu.VMEM((pattern.shape[0], lanes), i32),
+        pltpu.VMEM((sites, lanes), i32),
+        pltpu.VMEM((sites, lanes), i32),
+        pltpu.VMEM((3, half_rows, lanes), i32),
+        pltpu.VMEM((2 * half_rows, LANES), i32),
+        pltpu.SMEM((2 * half_rows, LANES), i32),
+        dma((8,)),
+        dma((2, groups, CHUNKS)),
+        dma((groups, CHUNKS)),
+        dma((groups, CHUNKS)),
+        dma((groups, CHUNKS)),
+        dma((chips,)),
+        dma((chips,)),
+        dma((CHUNKS, chips)),
+        dma((groups, CHUNKS, chips)),
+        dma((scens, sites)),
+        dma((groups, scens, sites)),
+        dma((groups, scens)),
+        dma((scens, groups)),
+        dma((2, scens, groups)),
+        pltpu.SemaphoreType.REGULAR((max(chips.bit_length() - 2, 1),)),
+    ]
+    taken = sum(
+        math.prod(ref.shape) * ref.dtype.itemsize
+        for ref in scratch
+        if ref.memory_space == pltpu.VMEM
+    )
+    limit = min(taken + taken // 16 + VMEM_MARGIN, VMEM_LIMIT)
     near, far = pl.pallas_call(
         functools.partial(kernel, chips, groups, slots, hours),
         out_shape=[jax.ShapeDtypeStruct((buses // sites, width), f32)] * 2,
         in_specs=[anywhere] * 7,
         out_specs=[whole] * 2,
-        scratch_shapes=[
-            pltpu.VMEM(pattern.shape, i32),
-            pltpu.VMEM(temporal.shape, bf16),
-            pltpu.VMEM((capacity.size // LANES, LANES), f32),
-            pltpu.VMEM((spread.size // LANES, LANES), f32),
-            pltpu.VMEM((bus_map.size // LANES, LANES), i32),
-            pltpu.VMEM((groups, PAIR, width, depth), bf16),
-            pltpu.VMEM((PAIR * block_count, step, blk), bf16),
-            pltpu.VMEM((rows_here, nz, height, blk), bf16),
-            pltpu.VMEM((chips, each, blk, rows), bf16),
-            pltpu.VMEM((chips, each, blk, rows), bf16),
-            pltpu.VMEM((2, chips, step, rows), bf16),
-            pltpu.VMEM((2, step, rows), f32),
-            pltpu.VMEM((groups, CHUNKS, chips, step, rows), bf16),
-            pltpu.VMEM((width, rows), f32),
-            pltpu.VMEM((scens, sites, packed_rows, shared), bf16),
-            pltpu.VMEM((groups, scens, sites, packed_rows, shared), bf16),
-            pltpu.VMEM((groups, scens, packed_rows, shared), f32),
-            pltpu.VMEM((scens, groups, packed_rows, shared), f32),
-            pltpu.VMEM((2, scens, groups, packed_rows, shared), f32),
-            pltpu.VMEM((scens, packed_rows, shared), f32),
-            pltpu.VMEM((buses, rows), bf16),
-            pltpu.VMEM((1, rows), f32),
-            pltpu.VMEM((1, rows), f32),
-            pltpu.VMEM((pattern.shape[0], lanes), i32),
-            pltpu.VMEM((sites, lanes), i32),
-            pltpu.VMEM((sites, lanes), i32),
-            pltpu.VMEM((3, half_rows, lanes), i32),
-            pltpu.VMEM((2 * half_rows, LANES), i32),
-            pltpu.SMEM((2 * half_rows, LANES), i32),
-            dma((8,)),
-            dma((2, groups, CHUNKS)),
-            dma((groups, CHUNKS)),
-            dma((groups, CHUNKS)),
-            dma((groups, CHUNKS)),
-            dma((chips,)),
-            dma((chips,)),
-            dma((2, chips)),
-            dma((groups, CHUNKS, chips)),
-            dma((scens, sites)),
-            dma((groups, scens, sites)),
-            dma((groups, scens)),
-            dma((scens, groups)),
-            dma((2, scens, groups)),
-            pltpu.SemaphoreType.REGULAR((max(chips.bit_length() - 2, 1),)),
-        ],
+        scratch_shapes=scratch,
         compiler_params=pltpu.CompilerParams(
-            collective_id=0, has_side_effects=True, vmem_limit_bytes=VMEM_LIMIT
+            collective_id=0, has_side_effects=True, vmem_limit_bytes=limit
         ),
     )(
-        pattern,
-        normals.T,
-        factor,
-        temporal,
-        capacity.reshape(-1, LANES),
-        spread.reshape(-1, LANES),
-        bus_map.reshape(-1, LANES),
+        *(
+            pltpu.with_memory_space_constraint(x, pltpu.HBM)
+            for x in (
+                pattern,
+                normals.T,
+                factor,
+                temporal,
+                capacity.reshape(-1, LANES),
+                spread.reshape(-1, LANES),
+                bus_map.reshape(-1, LANES),
+            )
+        )
     )
     return near + far
 

time: 136 us -> 131 us (0.963)
  Pallas kernels: 134 us -> 130 us
    pallas_call x1, Pallas kernels: 134 us -> 130 us  [shards(): pl.pallas_call(functools.partial(kernel, chips, groups, slots, hours), ou...]
where the time goes in v2:
time: 131 us
  Pallas kernels  130 us (99%)
    pallas_call x1, Pallas kernels, shards(): pl.pallas_call(functools.partial(kernel, chips, groups, slots, hours), ou...  130 us

profile of v2, /device:TPU:0, one launch (start us, length us, event | category | flops | bytes accessed | tf_op | source)
XLA Modules:
  0.0 130.9 jit_solution(16993564552537583940)
XLA Ops:
  0.0 130.3 %shard_map.73 = (f32[64,336]{1,0:T(8,128)S(1)}, f32[64,336]{1,0:T(8,128)S(1)}) custom-call(s32[32,40]{1,0:T(8,128)} %pattern_hbm.1, bf16[336,2560]{1,0:T(8,128)(2,1)} %bitcast.4, bf16[4,40,64,256]{3,2,1,0:T(8,128)(2,1)} %f_ref.1, bf16[168,168]{1,0:T(8,128)(2,1)} %temporal_hbm.1, f32[8,128]{1,0:T(8,128)} %bitcast.6, f32[8,128]{1,0:T(8,128)} %bitcast.7, ...), custom_call_target="tpu_custom_call" | custom-call | tf_op jit(solution)/shard_map/pallas_call | solution.py:768
  130.3 0.7 add.3

commit v3 on v2

--- a/solution.py
+++ b/solution.py
@@ -378,7 +378,9 @@
     more = jnp.where(z < last - z, 1, -1)
 
     def group_at(p):
-        near = jnp.where(p % 2 == 1, -((p + 1) // 2), (p + 1) // 2)
+        late = jnp.logical_and(jnp.logical_and(z > 0, z < last), p >= last - 1)
+        p = jnp.where(late, 2 * last - 1 - p, p)
+        near = jnp.where(p % 2 == 1, -more, more) * ((p + 1) // 2)
         far = more * (p - fewer)
         return z + jnp.where(p <= 2 * fewer, near, far)
 
@@ -444,7 +446,7 @@
             bottom = pltpu.roll(bottom, share_of, 1)
         return jnp.where(side == 0, top, bottom)
 
-    def multiply(g, ch, slot):
+    def multiply(g, ch, slot, kept):
         size = bounds[ch + 1] - bounds[ch]
         shared_in(g, ch).wait_recv()
         for half in range(PAIR):
@@ -472,15 +474,15 @@
             return carry
 
         lax.fori_loop(1, chips, one, 0)
-        s_own[slot, 0:size, :] = product(q)
+        s_own[kept, 0:size, :] = product(q)
 
     def lane_of(p):
         return jnp.where(p == 1, 1, 0)
 
-    def finish(p, ch):
+    def finish(p, ch, spare=False):
         g = group_at(p)
         size = bounds[ch + 1] - bounds[ch]
-        total = s_own[ch, 0:size, :]
+        total = s_own[CHUNKS if spare else ch, 0:size, :]
         for e in range(1, chips):
             s_copy(g, ch, 0, q, peer(e)).wait_recv()
             total = total + s_all[g, ch, peer(e), 0:size, :].astype(jnp.float32)
@@ -547,20 +549,20 @@
 
     final = CHUNKS - 1
 
-    def stage(p, ch):
+    def stage(p, ch, spare=False):
         g = group_at(p)
 
         @pl.when(p > 0)
         def _():
             free(g, ch, ch)
 
-        multiply(g, ch, ch)
+        multiply(g, ch, ch, CHUNKS if spare else ch)
 
     def position(p, carry):
         for ch in range(CHUNKS):
             if ch == final:
 
-                @pl.when(p != 1)
+                @pl.when(jnp.logical_or(p != 1, inner(z)))
                 def _():
                     stage(p, ch)
 
@@ -572,7 +574,8 @@
                     back = at // CHUNKS
                     ready = p >= back
                     if done_in(s) == final:
-                        ready = jnp.logical_and(ready, p != 1 + back)
+                        natural = jnp.logical_or(p != 1 + back, inner(z))
+                        ready = jnp.logical_and(ready, natural)
 
                     @pl.when(ready)
                     def _():
@@ -582,7 +585,7 @@
                 finish(p, ch - 1)
             else:
 
-                @pl.when(jnp.logical_and(p > 0, p != 2))
+                @pl.when(jnp.logical_and(p > 0, jnp.logical_or(p != 2, inner(z))))
                 def _():
                     finish(p - 1, final)
 
@@ -608,23 +611,30 @@
         return carry
 
     lax.fori_loop(0, groups, position, 0)
-    finish(last, final)
 
     @pl.when(is_end(z))
     def _():
         arrivals(1, final)
-
+        stage(1, final, True)
+
+    finish(last, final)
     for s in range(scens):
         if done_in(s) < final and done_in(s) + 3 >= CHUNKS:
             forward(last, s)
-    stage(1, final)
+
+    @pl.when(is_end(z))
+    def _():
+        finish(1, final, True)
+
     for s in range(scens):
         if done_in(s) == final:
             forward(last, s)
-    finish(1, final)
-    for s in range(scens):
-        if done_in(s) == final:
-            forward(1, s)
+
+    @pl.when(is_end(z))
+    def _():
+        for s in range(scens):
+            if done_in(s) == final:
+                forward(1, s)
 
     for g in range(groups):
         for ch in range(CHUNKS):
@@ -687,7 +697,7 @@
 
 def bounds_of(width):
     unit = width // 21
-    return [0, 8 * unit, 17 * unit, width]
+    return [0, 9 * unit, 18 * unit, width]
 
 
 def shards(normals, pattern, factor, temporal, capacity, spread, bus_map, buses):
@@ -725,7 +735,7 @@
         pltpu.VMEM((chips, each, blk, rows), bf16),
         pltpu.VMEM((chips, each, blk, rows), bf16),
         pltpu.VMEM((CHUNKS, chips, step, rows), bf16),
-        pltpu.VMEM((CHUNKS, step, rows), f32),
+        pltpu.VMEM((CHUNKS + 1, step, rows), f32),
         pltpu.VMEM((groups, CHUNKS, chips, step, rows), bf16),
         pltpu.VMEM((2, width, rows), f32),
         pltpu.VMEM((scens, sites, packed_rows, shared), bf16),

time: 131 us -> 131 us (level)
  no operation moved by 1% of the time
where the time goes in v3:
time: 131 us
  Pallas kernels  130 us (99%)
    pallas_call x1, Pallas kernels, shards(): pl.pallas_call(functools.partial(kernel, chips, groups, slots, hours), ou...  130 us

profile of v3, /device:TPU:0, one launch (start us, length us, event | category | flops | bytes accessed | tf_op | source)
XLA Modules:
  0.0 130.8 jit_solution(10306656450942927381)
XLA Ops:
  0.0 130.2 %shard_map.73 = (f32[64,336]{1,0:T(8,128)S(1)}, f32[64,336]{1,0:T(8,128)S(1)}) custom-call(s32[32,40]{1,0:T(8,128)} %pattern_hbm.1, bf16[336,2560]{1,0:T(8,128)(2,1)} %bitcast.4, bf16[4,40,64,256]{3,2,1,0:T(8,128)(2,1)} %f_ref.1, bf16[168,168]{1,0:T(8,128)(2,1)} %temporal_hbm.1, f32[8,128]{1,0:T(8,128)} %bitcast.6, f32[8,128]{1,0:T(8,128)} %bitcast.7, ...), custom_call_target="tpu_custom_call" | custom-call | tf_op jit(solution)/shard_map/pallas_call | solution.py:778
  130.2 0.7 add.3

commit v4 on v3

--- a/solution.py
+++ b/solution.py
@@ -102,8 +102,16 @@
 
     barrier = pltpu.get_barrier_semaphore()
 
+    def flip(i, mask, count):
+        total, bit = 0, 1
+        while bit < count:
+            a, b = (i // bit) % 2, (mask // bit) % 2
+            total = total + bit * (a + b - 2 * a * b)
+            bit *= 2
+        return total
+
     def peer(e):
-        return (q + e) % chips
+        return flip(q, chips - e, chips)
 
     def greet(device):
         pl.semaphore_signal(barrier, inc=1, device_id=device, device_id_type=MESH)
@@ -133,77 +141,6 @@
     ]
     for load in loads:
         load.start()
-    ends = jnp.where(z < last, 1, 0) + jnp.where(z > 0, 1, 0)
-    pl.semaphore_wait(barrier, 1 + len(bits) + ends)
-
-    def piece(ch):
-        return pl.ds(bounds[ch], bounds[ch + 1] - bounds[ch])
-
-    def hop(g, ch, up, source=None):
-        part = z_all.at[g, c, piece(ch)]
-        return pltpu.make_async_remote_copy(
-            src_ref=part if source is None else source,
-            dst_ref=part,
-            send_sem=zsend.at[up, g, ch],
-            recv_sem=zrecv.at[g, ch],
-            device_id=(k, z + 1 if up else z - 1),
-            device_id_type=MESH,
-        )
-
-    def share(g, ch, source=None):
-        part = z_all.at[g, c, piece(ch)]
-        return pltpu.make_async_remote_copy(
-            src_ref=part if source is None else source,
-            dst_ref=part,
-            send_sem=psend.at[g, ch],
-            recv_sem=precv.at[g, ch],
-            device_id=(other, z),
-            device_id_type=MESH,
-        )
-
-    def came_in(g, ch):
-        part = z_all.at[g, c, piece(ch)]
-        return pltpu.make_async_remote_copy(
-            src_ref=part,
-            dst_ref=part,
-            send_sem=psend.at[g, ch],
-            recv_sem=zrecv.at[g, ch],
-            device_id=(other, z),
-            device_id_type=MESH,
-        )
-
-    def shared_in(g, ch):
-        part = z_all.at[g, 1 - c, piece(ch)]
-        return pltpu.make_async_remote_copy(
-            src_ref=part,
-            dst_ref=part,
-            send_sem=psend.at[g, ch],
-            recv_sem=precv.at[g, ch],
-            device_id=(other, z),
-            device_id_type=MESH,
-        )
-
-    for ch in range(CHUNKS):
-        own = z_ref.at[piece(ch)]
-        late = ch == CHUNKS - 1
-
-        @pl.when(z < (last - 1 if late else last))
-        def _():
-            hop(z, ch, 1, own).start()
-
-        @pl.when(z > (1 if late else 0))
-        def _():
-            hop(z, ch, 0, own).start()
-
-    for ch in range(CHUNKS):
-        share(z, ch, z_ref.at[piece(ch)]).start()
-
-    for i, bit in enumerate(bits[:-1]):
-        pl.semaphore_signal(
-            meet.at[i], inc=1, device_id=(across(bit) * PAIR + c, z), device_id_type=MESH
-        )
-        pl.semaphore_wait(meet.at[i], 1)
-
     z_load = pltpu.make_async_copy(z_ref, z_all.at[z, c], local_sem.at[0])
     z_load.start()
     f_load = pltpu.make_async_copy(f_ref, f_raw, local_sem.at[1])
@@ -261,6 +198,78 @@
     t_load = pltpu.make_async_copy(tables, scalars, local_sem.at[2])
     t_load.start()
 
+    ends = jnp.where(z < last, 1, 0) + jnp.where(z > 0, 1, 0)
+    pl.semaphore_wait(barrier, 1 + len(bits) + ends)
+
+    def piece(ch):
+        return pl.ds(bounds[ch], bounds[ch + 1] - bounds[ch])
+
+    def hop(g, ch, up, source=None):
+        part = z_all.at[g, c, piece(ch)]
+        return pltpu.make_async_remote_copy(
+            src_ref=part if source is None else source,
+            dst_ref=part,
+            send_sem=zsend.at[up, g, ch],
+            recv_sem=zrecv.at[g, ch],
+            device_id=(k, z + 1 if up else z - 1),
+            device_id_type=MESH,
+        )
+
+    def share(g, ch, source=None):
+        part = z_all.at[g, c, piece(ch)]
+        return pltpu.make_async_remote_copy(
+            src_ref=part if source is None else source,
+            dst_ref=part,
+            send_sem=psend.at[g, ch],
+            recv_sem=precv.at[g, ch],
+            device_id=(other, z),
+            device_id_type=MESH,
+        )
+
+    def came_in(g, ch):
+        part = z_all.at[g, c, piece(ch)]
+        return pltpu.make_async_remote_copy(
+            src_ref=part,
+            dst_ref=part,
+            send_sem=psend.at[g, ch],
+            recv_sem=zrecv.at[g, ch],
+            device_id=(other, z),
+            device_id_type=MESH,
+        )
+
+    def shared_in(g, ch):
+        part = z_all.at[g, 1 - c, piece(ch)]
+        return pltpu.make_async_remote_copy(
+            src_ref=part,
+            dst_ref=part,
+            send_sem=psend.at[g, ch],
+            recv_sem=precv.at[g, ch],
+            device_id=(other, z),
+            device_id_type=MESH,
+        )
+
+    for ch in range(CHUNKS):
+        own = z_ref.at[piece(ch)]
+        late = ch == CHUNKS - 1
+
+        @pl.when(z < (last - 1 if late else last))
+        def _():
+            hop(z, ch, 1, own).start()
+
+        @pl.when(z > (1 if late else 0))
+        def _():
+            hop(z, ch, 0, own).start()
+
+    for ch in range(CHUNKS):
+        share(z, ch, z_ref.at[piece(ch)]).start()
+
+    for i, bit in enumerate(bits[:-1]):
+        pl.semaphore_signal(
+            meet.at[i], inc=1, device_id=(across(bit) * PAIR + c, z), device_id_type=MESH
+        )
+        pl.semaphore_wait(meet.at[i], 1)
+
+
     narrow = capacity_ref.shape[1]
     narrow_lane = lax.broadcasted_iota(jnp.int32, (8, narrow), 1)
     offset = z * height
@@ -395,18 +404,19 @@
             device_id_type=MESH,
         )
 
-    def b_copy(g, s, target, source):
+    def b_copy(g, s, target, source, slot=None):
+        slot = s if slot is None else slot
         return pltpu.make_async_remote_copy(
-            src_ref=b_send.at[s, target],
+            src_ref=b_send.at[slot, target],
             dst_ref=b_all.at[g, s, source],
-            send_sem=bsend.at[s, target],
+            send_sem=bsend.at[slot, target],
             recv_sem=brecv.at[g, s, source],
             device_id=(target, z),
             device_id_type=MESH,
         )
 
     def seat(e):
-        return (k + e) % sites
+        return flip(k, sites - e, sites)
 
     def c_copy(g, s, source):
         return pltpu.make_async_remote_copy(
@@ -501,18 +511,21 @@
                 preferred_element_type=jnp.float32,
             )
 
-            @pl.when(p > 0)
-            def _():
-                for e in range(1, sites):
-                    b_copy(g, s, seat(e), k).wait_send()
+            slot = scens if spare else s
+            if not spare:
+
+                @pl.when(p > 0)
+                def _():
+                    for e in range(1, sites):
+                        b_copy(g, s, seat(e), k).wait_send()
 
             for i in range(chips):
                 block = sums[:, i * shared : (i + 1) * shared]
                 for core in range(PAIR):
-                    b_send[s, i * PAIR + core] = pack(block, core).astype(b_send.dtype)
+                    b_send[slot, i * PAIR + core] = pack(block, core).astype(b_send.dtype)
             for e in range(1, sites):
-                b_copy(g, s, seat(e), k).start()
-            b_all[g, s, k] = b_send[s, k]
+                b_copy(g, s, seat(e), k, slot).start()
+            b_all[g, s, k] = b_send[slot, k]
 
     def forward(p, s):
         g = group_at(p)
@@ -690,6 +703,12 @@
     for s in range(scens):
         for e in range(1, sites):
             b_copy(z, s, seat(e), k).wait_send()
+
+    @pl.when(is_end(z))
+    def _():
+        for e in range(1, sites):
+            b_copy(z, 0, seat(e), k, scens).wait_send()
+
     for s in range(scens):
         for d in range(1, groups):
             c_copy((z + d) % groups, s, z).wait_send()
@@ -738,7 +757,7 @@
         pltpu.VMEM((CHUNKS + 1, step, rows), f32),
         pltpu.VMEM((groups, CHUNKS, chips, step, rows), bf16),
         pltpu.VMEM((2, width, rows), f32),
-        pltpu.VMEM((scens, sites, packed_rows, shared), bf16),
+        pltpu.VMEM((scens + 1, sites, packed_rows, shared), bf16),
         pltpu.VMEM((groups, scens, sites, packed_rows, shared), bf16),
         pltpu.VMEM((groups, scens, packed_rows, shared), f32),
         pltpu.VMEM((scens, groups, packed_rows, shared), f32),
@@ -762,7 +781,7 @@
         dma((chips,)),
         dma((CHUNKS, chips)),
         dma((groups, CHUNKS, chips)),
-        dma((scens, sites)),
+        dma((scens + 1, sites)),
         dma((groups, scens, sites)),
         dma((groups, scens)),
         dma((scens, groups)),

time: 131 us -> 131 us (level)
  no operation moved by 1% of the time
where the time goes in v4:
time: 131 us
  Pallas kernels  130 us (99%)
    pallas_call x1, Pallas kernels, shards(): pl.pallas_call(functools.partial(kernel, chips, groups, slots, hours), ou...  130 us

profile of v4, /device:TPU:0, one launch (start us, length us, event | category | flops | bytes accessed | tf_op | source)
XLA Modules:
  0.0 131.1 jit_solution(14870940836027538823)
XLA Ops:
  0.0 130.5 %shard_map.73 = (f32[64,336]{1,0:T(8,128)S(1)}, f32[64,336]{1,0:T(8,128)S(1)}) custom-call(s32[32,40]{1,0:T(8,128)} %pattern_hbm.1, bf16[336,2560]{1,0:T(8,128)(2,1)} %bitcast.4, bf16[4,40,64,256]{3,2,1,0:T(8,128)(2,1)} %f_ref.1, bf16[168,168]{1,0:T(8,128)(2,1)} %temporal_hbm.1, f32[8,128]{1,0:T(8,128)} %bitcast.6, f32[8,128]{1,0:T(8,128)} %bitcast.7, ...), custom_call_target="tpu_custom_call" | custom-call | tf_op jit(solution)/shard_map/pallas_call | solution.py:797
  130.5 0.7 add.3

commit v5 on v3

--- a/solution.py
+++ b/solution.py
@@ -102,8 +102,16 @@
 
     barrier = pltpu.get_barrier_semaphore()
 
+    def flip(i, mask, count):
+        total, bit = 0, 1
+        while bit < count:
+            a, b = (i // bit) % 2, (mask // bit) % 2
+            total = total + bit * (a + b - 2 * a * b)
+            bit *= 2
+        return total
+
     def peer(e):
-        return (q + e) % chips
+        return flip(q, chips - e, chips)
 
     def greet(device):
         pl.semaphore_signal(barrier, inc=1, device_id=device, device_id_type=MESH)
@@ -406,7 +414,7 @@
         )
 
     def seat(e):
-        return (k + e) % sites
+        return flip(k, sites - e, sites)
 
     def c_copy(g, s, source):
         return pltpu.make_async_remote_copy(

time: 131 us -> 131 us (level)
  no operation moved by 1% of the time
where the time goes in v5:
time: 131 us
  Pallas kernels  130 us (99%)
    pallas_call x1, Pallas kernels, shards(): pl.pallas_call(functools.partial(kernel, chips, groups, slots, hours), ou...  130 us

profile of v5, /device:TPU:0, one launch (start us, length us, event | category | flops | bytes accessed | tf_op | source)
XLA Modules:
  0.0 130.9 jit_solution(13508684396739895581)
XLA Ops:
  0.0 130.2 %shard_map.73 = (f32[64,336]{1,0:T(8,128)S(1)}, f32[64,336]{1,0:T(8,128)S(1)}) custom-call(s32[32,40]{1,0:T(8,128)} %pattern_hbm.1, bf16[336,2560]{1,0:T(8,128)(2,1)} %bitcast.4, bf16[4,40,64,256]{3,2,1,0:T(8,128)(2,1)} %f_ref.1, bf16[168,168]{1,0:T(8,128)(2,1)} %temporal_hbm.1, f32[8,128]{1,0:T(8,128)} %bitcast.6, f32[8,128]{1,0:T(8,128)} %bitcast.7, ...), custom_call_target="tpu_custom_call" | custom-call | tf_op jit(solution)/shard_map/pallas_call | solution.py:786
  130.2 0.7 add.3
